TPU v7x, 512 devices: a whole 4x8x8 slice. The times are simulated.
512 devices in a mesh: rows: 32 (over x, z), cols: 16 (over y, core).
Axes of the slice: x: 4, y: 8, z: 8, core: 2. Of those that a mesh axis runs over, the one named last changes fastest.
Arguments:
- points: float32 [3, 131072], P(None, 'rows'), as said below
- targets: float32 [16, 131072], P(None, 'rows'), may hold values from -6 to 6
- landmarks: int32 [256], replicated, may hold values from 0 to 131071
- neighbours: int32 [1024, 18], P('rows'), may hold values from 0 to 1023, as said below
- counts: int32 [1024], P('rows'), may hold values from 1 to 18
- core_inverse: float32 [256, 256], replicated, as said below
Outputs:
- solution: float32 [16, 131072], P(None, 'rows')
- residual: float32 [16, 131072], P(None, 'rows')
Inputs may be any that keep to these rules, and one draw needn't show every extreme that they name: `neighbours`: for block b the first counts[b] entries are distinct blocks in ascending order, b among them, each within 12 blocks of b; b lists c exactly when c lists b; the remaining slots hold b. `points`: points of blocks that do not list each other are farther apart than 1. `core_inverse`: Symmetric; each diagonal entry exceeds the sum of the magnitudes of the other entries of its row.
All inputs are finite; a program needn't handle non-finite values.
Results may differ from a plain program's by a relative error of at most 0.0003.
Values sent between devices are 32-bit elements; how exact they have to be, the bound alone decides.
A program may use at most 64 MiB of HBM per device.

v0:
```python
import jax
import jax.numpy as jnp
from jax import lax
from jax.sharding import PartitionSpec as P

MOST = 6
ITERS = 2
kernel_scale = 0.03125
ridge_shift = 1.0
tile_group = 32


def extended(cells, sides, width):
    for axis, dim in sides:
        count = lax.axis_size(axis)
        ends = count - 1
        head = lax.slice_in_dim(cells, 0, width, axis=dim)
        tail = lax.slice_in_dim(cells, cells.shape[dim] - width, cells.shape[dim], axis=dim)
        cells = jnp.concatenate(
            [
                lax.ppermute(tail, axis, [(i, (i + 1) % count) for i in range(ends)]),
                cells,
                lax.ppermute(head, axis, [((i + 1) % count, i) for i in range(ends)]),
            ],
            axis=dim,
        )
    return cells


def wendland(squared):
    distance = jnp.sqrt(squared)
    remain = jnp.maximum(1.0 - distance, 0.0)
    return remain * remain * remain * remain * (4.0 * distance + 1.0)


def squared_gap(first_pts, second_pts):
    offsets = first_pts[:, :, None] - second_pts[:, None, :]
    return jnp.sum(offsets * offsets, axis=0)


def tile_products(vector_halo, point_halo, row_points, nearby, amounts, last_tile):
    block_count = row_points.shape[1]
    block_width = row_points.shape[2]
    slot_count = nearby.shape[1]
    tile_ends = jnp.cumsum(amounts)
    tile_starts = tile_ends - amounts
    lane_ids = jnp.arange(tile_group, dtype=jnp.int32)
    block_ids = jnp.arange(block_count, dtype=jnp.int32)
    turn_count = (last_tile + tile_group - 1) // tile_group

    def advance(turn_index, running):
        position = turn_index * tile_group + lane_ids
        inside = position < last_tile
        owner_block = jnp.sum((tile_ends[None, :] <= position[:, None]).astype(jnp.int32), axis=1)
        owner_block = jnp.minimum(owner_block, block_count - 1)
        column = jnp.clip(position - tile_starts[owner_block], 0, slot_count - 1)
        partner = nearby[owner_block, column]
        row_side = row_points[:, owner_block]
        col_side = point_halo[:, partner]
        offsets = row_side[:, :, :, None] - col_side[:, :, None, :]
        kernel_tiles = wendland(jnp.sum(offsets * offsets, axis=0)) * inside[:, None, None].astype(
            jnp.float32
        )
        contrib = jnp.einsum(
            "ogn,gmn->ogm", vector_halo[:, partner], kernel_tiles, precision=lax.Precision.HIGHEST
        )
        placing = ((owner_block[:, None] == block_ids[None, :]) & inside[:, None]).astype(
            jnp.float32
        )
        return running + jnp.einsum(
            "ogm,gb->obm", contrib, placing, precision=lax.Precision.HIGHEST
        )

    start_total = jnp.zeros((vector_halo.shape[0], block_count, block_width), jnp.float32)
    return lax.fori_loop(0, turn_count, advance, start_total)


def body(points, targets, landmarks, neighbours, counts, core_inverse):
    col_count = lax.axis_size("cols")
    row_index = lax.axis_index("rows")
    col_index = lax.axis_index("cols")
    block_count = neighbours.shape[0]
    slab_points = points.shape[1]
    block_width = slab_points // block_count
    share_blocks = block_count // col_count
    share_points = share_blocks * block_width
    outputs_count = targets.shape[0]
    reach = 2 * MOST
    first_block = row_index * block_count
    local_ids = landmarks - row_index * slab_points
    present = (local_ids >= 0) & (local_ids < slab_points)
    picked = jnp.take(points, jnp.clip(local_ids, 0, slab_points - 1), axis=1) * present[
        None, :
    ].astype(jnp.float32)
    landmark_coords = lax.psum(picked, "rows")
    share_start = col_index * share_points
    own_points = lax.dynamic_slice_in_dim(points, share_start, share_points, 1)
    landmark_kernel = kernel_scale * wendland(squared_gap(landmark_coords, own_points))

    def precondition_share(residual_share):
        projected = jnp.dot(residual_share, landmark_kernel.T, precision=lax.Precision.HIGHEST)
        projected = lax.psum(projected, ("rows", "cols"))
        weights = jnp.dot(projected, core_inverse, precision=lax.Precision.HIGHEST)
        shared = residual_share - jnp.dot(weights, landmark_kernel, precision=lax.Precision.HIGHEST)
        product = lax.psum(jnp.sum(residual_share * shared, axis=1), ("rows", "cols"))
        return (shared, product)

    point_halo = extended(points, (("rows", 1),), reach * block_width)
    point_halo = point_halo.reshape(3, -1, block_width)
    nearby = neighbours - (first_block - reach)

    def share_of(vector):
        return lax.dynamic_slice_in_dim(vector, share_start, share_points, 1)

    def precondition(residual):
        shared, product = precondition_share(share_of(residual))
        return (lax.all_gather(shared, "cols", axis=1, tiled=True), product)

    solution = jnp.zeros_like(targets)
    residual = targets
    preconditioned, current = precondition(residual)
    direction = preconditioned
    for iteration in range(ITERS):
        vector_halo = extended(direction, (("rows", 1),), reach * block_width)
        vector_halo = vector_halo.reshape(outputs_count, -1, block_width)
        own_lists = lax.dynamic_slice_in_dim(nearby, col_index * share_blocks, share_blocks, 0)
        amounts = lax.dynamic_slice_in_dim(counts, col_index * share_blocks, share_blocks, 0)
        rows_here = own_points.reshape(3, share_blocks, block_width)
        tile_total = jnp.sum(amounts)
        partial_rows = tile_products(
            vector_halo, point_halo, rows_here, own_lists, amounts, tile_total
        )
        operate_product = lax.all_gather(
            partial_rows.reshape(outputs_count, share_points), "cols", axis=1, tiled=True
        )
        applied = kernel_scale * operate_product + ridge_shift * direction
        curvature_part = jnp.sum(share_of(direction) * share_of(applied), axis=1)
        step_size = current / lax.psum(curvature_part, ("rows", "cols"))
        solution = solution + step_size[:, None] * direction
        residual = residual - step_size[:, None] * applied
        if iteration + 1 < ITERS:
            preconditioned, following = precondition(residual)
            direction = preconditioned + (following / current)[:, None] * direction
            current = following
    solution, residual = (solution, residual)
    return (solution, residual)


def solution(mesh):
    placed = (P(None, "rows"), P(None, "rows"), P(), P("rows", None), P("rows"), P())
    return jax.shard_map(
        body,
        mesh=mesh,
        in_specs=placed,
        out_specs=(P(None, "rows"), P(None, "rows")),
        check_vma=False,
    )
```

profile of v0, /device:TPU:1, one launch (start us, length us, event | category | flops | bytes accessed | tf_op | source)
XLA Modules:
  0.0 767.7 jit_solution(12587315131149481955)
XLA Ops:
  0.7 0.8 fusion.98
  1.5 4.8 collective-permute-start
  6.3 1.3 collective-permute-start.1
  7.6 1.5 copy.37
  9.2 0.7 gather_fusion.8
  10.1 121.2 %psum.49 = f32[3,256]{0,1:T(8,128)S(1)} all-reduce(f32[3,256]{0,1:T(8,128)S(1)} %multiply_bitcast_fusion), channel_id=1, replica_groups=mesh['rows'=32,'cols'=16] {'rows'}, use_global_device_ids=true, to_apply=%region_0.1 | all-reduce | flops 768 | bytes 6144 | tf_op jit(solution)/shard_map/psum | solution.py:95
  131.6 0.4 fusion.84
  132.0 124.0 %psum.50 = f32[16,256]{1,0:T(8,128)S(1)} all-reduce(f32[16,256]{1,0:T(8,128)S(1)} %fusion.84), channel_id=1, replica_groups=mesh['rows'=32,'cols'=16] {'rows','cols'}, use_global_device_ids=true, to_apply=%region_2.3 | all-reduce | flops 4096 | bytes 32768 | tf_op jit(solution)/shard_map/psum | solution.py:102
  256.2 0.5 multiply_reduce_fusion.6
  256.7 16.2 %all_gather.12 = f32[16,4096]{1,0:T(8,128)S(1)} all-gather(f32[16,256]{1,0:T(8,128)S(1)} %get-tuple-element.306), channel_id=1, replica_groups=mesh['rows'=32,'cols'=16] {'cols'}, dimensions={1}, use_global_device_ids=true | all-gather | bytes 278528 | tf_op jit(solution)/shard_map/all_gather | solution.py:117
  272.9 2.8 collective-permute-start.2
  275.7 1.3 collective-permute-start.3
  277.3 0.8 bitcast_subtract_fusion
  279.0 2.5 collective-permute-done.3
  281.6 12.1 %while.22 = (s32[]{:T(128)}, f32[16,2,128]{2,1,0:T(2,128)S(1)}, s32[]{:T(128)}, s32[2]{0:T(128)S(1)}, s32[]{:T(128)}, /*index=5*/f32[3,2,128]{2,0,1:T(4,128)S(1)...) while((s32[]{:T(128)}, f32[16,2,128]{2,1,0:T(2,128)S(1)}, ...), condition=%wide.region_10.11_spmd.clone, body=%wide.region_7.10_spmd.clone.sunk | while | flops 111156288 | bytes 6040561 | solution.py:75
  281.7 0.6 fusion.135
  282.3 1.3 fusion.136
  283.6 0.8 gather_fusion
  284.4 0.7 fusion.138
  285.1 0.6 gather_fusion.2
  285.7 0.6 gather_fusion.1
  286.4 0.6 gather_fusion.3
  287.0 2.1 multiply_reduce_fusion.9
  289.0 4.3 fusion.139
  293.7 16.3 %all_gather.13 = f32[16,4096]{1,0:T(8,128)S(1)} all-gather(f32[16,256]{1,0:T(8,128)S(1)} %bitcast.164), channel_id=1, replica_groups=mesh['rows'=32,'cols'=16] {'cols'}, dimensions={1}, use_global_device_ids=true | all-gather | bytes 278528 | tf_op jit(solution)/shard_map/all_gather | solution.py:133
  310.1 104.1 %all-reduce = (f32[16]{0:T(128)S(1)}, f32[16]{0:T(128)S(1)}) all-reduce(f32[16]{0:T(128)S(1)} %get-tuple-element.305, f32[16]{0:T(128)S(1)} %multiply_reduce_fusion.5), channel_id=1, replica_groups=mesh['rows'=32,'cols'=16] {'rows','cols'}, use_global_device_ids=true, to_apply=%region_4.5 | all-reduce | flops 32 | bytes 256 | tf_op jit(solution)/shard_map/psum | solution.py:105
  414.3 0.4 fusion.82
  414.7 94.7 %psum.53 = f32[16,256]{1,0:T(8,128)S(1)} all-reduce(f32[16,256]{1,0:T(8,128)S(1)} %fusion.82), channel_id=1, replica_groups=mesh['rows'=32,'cols'=16] {'rows','cols'}, use_global_device_ids=true, to_apply=%region_13.14 | all-reduce | flops 4096 | bytes 32768 | tf_op jit(solution)/shard_map/psum | solution.py:102
  509.6 0.5 multiply_reduce_fusion.4
  510.1 95.3 %psum.54 = f32[16]{0:T(128)S(1)} all-reduce(f32[16]{0:T(128)S(1)} %get-tuple-element.307), channel_id=1, replica_groups=mesh['rows'=32,'cols'=16] {'rows','cols'}, use_global_device_ids=true, to_apply=%region_15.16 | all-reduce | flops 16 | bytes 128 | tf_op jit(solution)/shard_map/psum | solution.py:105
  605.4 18.2 %all_gather.14 = f32[16,4096]{1,0:T(8,128)S(1)} all-gather(f32[16,256]{1,0:T(8,128)S(1)} %get-tuple-element.308), channel_id=1, replica_groups=mesh['rows'=32,'cols'=16] {'cols'}, dimensions={1}, use_global_device_ids=true | all-gather | bytes 278528 | tf_op jit(solution)/shard_map/all_gather | solution.py:117
  623.7 1.7 collective-permute-start.4
  625.4 1.3 collective-permute-start.5
  626.7 0.7 collective-permute-done.4
  627.4 4.6 collective-permute-done.5
  632.1 12.0 %while.23 = (s32[]{:T(128)}, f32[16,2,128]{2,1,0:T(2,128)S(1)}, s32[]{:T(128)}, s32[2]{0:T(128)S(1)}, s32[]{:T(128)}, /*index=5*/f32[3,2,128]{2,0,1:T(4,128)S(1)...) while((s32[]{:T(128)}, f32[16,2,128]{2,1,0:T(2,128)S(1)}, ...), condition=%wide.region_19.20_spmd.clone, body=%wide.region_16.19_spmd.clone.sunk | while | flops 111156288 | bytes 6040561 | solution.py:75
  632.2 0.6 fusion.146
  632.8 1.3 fusion.147
  634.1 0.8 gather_fusion.4
  634.8 0.7 fusion.149
  635.6 0.6 gather_fusion.6
  636.2 0.6 gather_fusion.5
  636.8 0.6 gather_fusion.7
  637.4 2.1 multiply_reduce_fusion.10
  639.5 4.3 fusion.150
  644.1 17.1 %all_gather.15 = f32[16,4096]{1,0:T(8,128)S(1)} all-gather(f32[16,256]{1,0:T(8,128)S(1)} %bitcast.165), channel_id=1, replica_groups=mesh['rows'=32,'cols'=16] {'cols'}, dimensions={1}, use_global_device_ids=true | all-gather | bytes 278528 | tf_op jit(solution)/shard_map/all_gather | solution.py:133
  661.4 105.4 %psum.55 = f32[16]{0:T(128)S(1)} all-reduce(f32[16]{0:T(128)S(1)} %multiply_reduce_fusion.3), channel_id=1, replica_groups=mesh['rows'=32,'cols'=16] {'rows','cols'}, use_global_device_ids=true, to_apply=%region_21.22 | all-reduce | flops 16 | bytes 128 | tf_op jit(solution)/shard_map/psum | solution.py:138
  766.8 0.9 multiply_subtract_fusion
  (64 shorter events, 2.8 us)
Async XLA Ops:
  0.6 255.4 %copy-start = (f32[256,256]{1,0:T(8,128)S(1)}, f32[256,256]{1,0:T(8,128)}, u32[]{:S(2)}) copy-start(f32[256,256]{1,0:T(8,128)} %param.15) | copy-start | bytes 786436
  0.6 8.5 %copy-start.1 = (f32[3,4096]{1,0:T(4,128)S(1)}, f32[3,4096]{1,0:T(4,128)}, u32[]{:S(2)}) copy-start(f32[3,4096]{1,0:T(4,128)} %param.10) | copy-start | bytes 147460
  0.7 8.5 %copy-start.4 = (s32[256]{0:T(256)S(1)}, s32[256]{0:T(256)}, u32[]{:S(2)}) copy-start(s32[256]{0:T(256)} %param.12) | copy-start | bytes 3076
  0.7 130.9 %copy-start.2 = (f32[16,4096]{1,0:T(8,128)S(1)}, f32[16,4096]{1,0:T(8,128)}, u32[]{:S(2)}) copy-start(f32[16,4096]{1,0:T(8,128)} %param.11) | copy-start | bytes 786436
  1.5 277.5 %collective-permute-start = (f32[3,1536]{1,0:T(4,128)S(1)}, f32[3,1536]{1,0:T(4,128)S(1)}, u32[]{:S(2)}, u32[]{:S(2)}) collective-permute-start(f32[3,1536]{1,0:T(4,128)S(1)} %get-tuple-element.298), channel_id=1, source_target_pairs={{0,16},{16,32},{32,48},{48,64},{64,80},{80,96},{96,112},{112,128},... | collective-permute-start | bytes 55304 | tf_op jit(solution)/shard_map/ppermute | solution.py:21
  6.3 272.6 %collective-permute-start.1 = (f32[3,1536]{1,0:T(4,128)S(1)}, f32[3,1536]{1,0:T(4,128)S(1)}, u32[]{:S(2)}, u32[]{:S(2)}) collective-permute-start(f32[3,1536]{1,0:T(4,128)S(1)} %get-tuple-element.299), channel_id=1, source_target_pairs={{16,0},{32,16},{48,32},{64,48},{80,64},{96,80},{112,96},{128,112},... | collective-permute-start | bytes 55304 | tf_op jit(solution)/shard_map/ppermute | solution.py:23
  9.1 267.9 %copy-start.5 = (s32[32]{0:T(128)S(1)}, s32[32]{0:T(128)}, u32[]{:S(2)}) copy-start(s32[32]{0:T(128)} %param.14) | copy-start | bytes 388
  9.1 269.0 %copy-start.3 = (s32[32,18]{0,1:T(8,128)S(1)}, s32[32,18]{0,1:T(8,128)}, u32[]{:S(2)}) copy-start(s32[32,18]{0,1:T(8,128)} %param.13) | copy-start | bytes 6916
  272.9 6.1 collective-permute-start.2
  275.7 5.8 collective-permute-start.3
  623.7 3.6 collective-permute-start.4
  625.4 6.6 collective-permute-start.5
where the time goes:
time: 769 us; the launch traced here: 768 us
  blocking collectives  713 us (93%)
  starting transfers between devices  13.1 us (2%)
  matrix products  11.3 us (1%)
  other arithmetic  11.2 us (1%)
  local copies, waits for them, and re-layouts  9.75 us (1%)
  waiting for transfers between devices  7.82 us (1%)
    psum x2, blocking collectives, precondition_share(): projected = lax.psum(projected, ('rows', 'cols'))  219 us
    psum x2, blocking collectives, precondition_share(): lax.psum(jnp.sum(residual_share * shared, axis=1), ('rows', 'cols'))  199 us
    psum x1, blocking collectives, body(): landmark_coords = lax.psum(picked, 'rows')  121 us
    psum x1, blocking collectives, body(): step_size = current / lax.psum(curvature_part, ('rows', 'cols'))  105 us
    all_gather x2, blocking collectives, precondition(): return (lax.all_gather(shared, 'cols', axis=1, tiled=True), product)  34.4 us
    all_gather x2, blocking collectives, body(): lax.all_gather(partial_rows.reshape(outputs_count, share_points), 'cols',...  33.5 us
  transfers between devices with their start and end apart: 6, of which 3 were waited for; matrix products, arithmetic and copies ran while one was open for 1% of the time, Pallas kernels for 0%

commit v1 on v0

--- a/solution.py
+++ b/solution.py
@@ -8,6 +8,15 @@
 kernel_scale = 0.03125
 ridge_shift = 1.0
 tile_group = 32
+
+
+def added_up(x, mesh_axis):
+    size = lax.axis_size(mesh_axis)
+    summed, hop = (x, 1)
+    while hop < size:
+        summed = summed + lax.ppermute(summed, mesh_axis, [(i, i ^ hop) for i in range(size)])
+        hop = 2 * hop
+    return summed
 
 
 def extended(cells, sides, width):
@@ -92,7 +101,7 @@
     picked = jnp.take(points, jnp.clip(local_ids, 0, slab_points - 1), axis=1) * present[
         None, :
     ].astype(jnp.float32)
-    landmark_coords = lax.psum(picked, "rows")
+    landmark_coords = added_up(picked, "rows")
     share_start = col_index * share_points
     own_points = lax.dynamic_slice_in_dim(points, share_start, share_points, 1)
     landmark_kernel = kernel_scale * wendland(squared_gap(landmark_coords, own_points))

time: 769 us -> 673 us (0.88)
  blocking collectives: 713 us -> 571 us
  starting transfers between devices: 13.1 us -> 37 us
  waiting for transfers between devices: 7.82 us -> 30.1 us
    psum x1 -> x0, blocking collectives: 121 us -> none  [body(): landmark_coords = lax.psum(picked, 'rows')]
    ppermute x0 -> x5, starting transfers between devices: none -> 23.9 us  [added_up(): lax.ppermute(summed, mesh_axis, [(i, i ^ hop) for i in range(size)])]
    psum x2, blocking collectives: 219 us -> 197 us  [precondition_share(): projected = lax.psum(projected, ('rows', 'cols'))]
    ppermute x0 -> x5, waiting for transfers between devices: none -> 20.4 us  [added_up(): lax.ppermute(summed, mesh_axis, [(i, i ^ hop) for i in range(size)])]
  transfers between devices with their start and end apart: 6 -> 11, of which waited for: 3 -> 9; matrix products, arithmetic and copies ran while one was open for 1% -> 1% of each run, Pallas kernels for 0% -> 0%
where the time goes in v1:
time: 673 us; the launch traced here: 672 us
  blocking collectives  571 us (85%)
  starting transfers between devices  37 us (5%)
  waiting for transfers between devices  30.1 us (4%)
  other arithmetic  11.4 us (2%)
  matrix products  11.3 us (2%)
  local copies, waits for them, and re-layouts  9.78 us (1%)
    psum x2, blocking collectives, precondition_share(): lax.psum(jnp.sum(residual_share * shared, axis=1), ('rows', 'cols'))  200 us
    psum x2, blocking collectives, precondition_share(): projected = lax.psum(projected, ('rows', 'cols'))  197 us
    psum x1, blocking collectives, body(): step_size = current / lax.psum(curvature_part, ('rows', 'cols'))  105 us
    all_gather x2, blocking collectives, precondition(): return (lax.all_gather(shared, 'cols', axis=1, tiled=True), product)  34.3 us
    all_gather x2, blocking collectives, body(): lax.all_gather(partial_rows.reshape(outputs_count, share_points), 'cols',...  33.5 us
    ppermute x5, starting transfers between devices, added_up(): lax.ppermute(summed, mesh_axis, [(i, i ^ hop) for i in range(size)])  23.9 us
    ppermute x5, waiting for transfers between devices, added_up(): lax.ppermute(summed, mesh_axis, [(i, i ^ hop) for i in range(size)])  20.4 us
  transfers between devices with their start and end apart: 11, of which 9 were waited for; matrix products, arithmetic and copies ran while one was open for 1% of the time, Pallas kernels for 0%

profile of v1, /device:TPU:1, one launch (start us, length us, event | category | flops | bytes accessed | tf_op | source)
XLA Modules:
  0.0 672.2 jit_solution(13217513233991936336)
XLA Ops:
  0.7 0.8 fusion.98
  1.5 4.8 collective-permute-start.5
  6.3 1.3 collective-permute-start.6
  7.6 1.5 copy.37
  9.2 0.7 gather_fusion.8
  10.1 4.6 collective-permute-start
  15.0 2.1 collective-permute-done
  17.2 7.6 %collective-permute-start.1 = (f32[3,256]{0,1:T(8,128)S(1)}, f32[3,256]{0,1:T(8,128)S(1)}, u32[]{:S(2)}, u32[]{:S(2)}) collective-permute-start(f32[3,256]{0,1:T(8,128)S(1)} %fusion.108), channel_id=1, source_target_pairs={{0,32},{16,48},{32,0},{48,16},{64,96},{80,112},{96,64},{112,80},{1... | collective-permute-start | bytes 9224 | tf_op jit(solution)/shard_map/ppermute | solution.py:17
  24.8 0.8 bitcast_subtract_fusion
  25.6 5.4 collective-permute-done.1
  30.9 4.6 collective-permute-start.2
  35.6 7.8 %collective-permute-done.2 = f32[3,256]{0,1:T(8,128)S(1)} collective-permute-done((f32[3,256]{0,1:T(8,128)S(1)}, f32[3,256]{0,1:T(8,128)S(1)}, u32[]{:S(2)}, u32[]{:S(2)}) %collective-permute-start.2) | collective-permute-done | bytes 3104 | tf_op jit(solution)/shard_map/ppermute | solution.py:17
  43.4 2.8 collective-permute-start.3
  46.2 2.9 collective-permute-done.3
  49.1 4.3 collective-permute-start.4
  54.3 2.3 collective-permute-done.4
  57.3 102.4 %psum.42 = f32[16,256]{1,0:T(8,128)S(1)} all-reduce(f32[16,256]{1,0:T(8,128)S(1)} %fusion.84), channel_id=1, replica_groups=mesh['rows'=32,'cols'=16] {'rows','cols'}, use_global_device_ids=true, to_apply=%region_1.2 | all-reduce | flops 4096 | bytes 32768 | tf_op jit(solution)/shard_map/psum | solution.py:111
  160.4 16.3 %all_gather.12 = f32[16,4096]{1,0:T(8,128)S(1)} all-gather(f32[16,256]{1,0:T(8,128)S(1)} %get-tuple-element.306), channel_id=1, replica_groups=mesh['rows'=32,'cols'=16] {'cols'}, dimensions={1}, use_global_device_ids=true | all-gather | bytes 278528 | tf_op jit(solution)/shard_map/all_gather | solution.py:126
  176.7 2.7 collective-permute-start.7
  179.4 1.3 collective-permute-start.8
  180.7 0.6 collective-permute-done.7
  181.4 3.8 collective-permute-done.8
  185.2 12.1 %while.22 = (s32[]{:T(128)}, f32[16,2,128]{2,1,0:T(2,128)S(1)}, s32[]{:T(128)}, s32[2]{0:T(128)S(1)}, s32[]{:T(128)}, /*index=5*/f32[3,2,128]{2,0,1:T(4,128)S(1)...) while((s32[]{:T(128)}, f32[16,2,128]{2,1,0:T(2,128)S(1)}, ...), condition=%wide.region_9.10_spmd.clone, body=%wide.region_6.9_spmd.clone.sunk | while | flops 111156288 | bytes 6040561 | solution.py:84
  185.4 0.6 fusion.136
  186.0 1.3 fusion.137
  187.3 0.8 gather_fusion
  188.1 0.7 fusion.139
  189.4 0.6 gather_fusion.1
  190.6 2.1 multiply_reduce_fusion.9
  192.7 4.3 fusion.140
  197.3 16.4 %all_gather.13 = f32[16,4096]{1,0:T(8,128)S(1)} all-gather(f32[16,256]{1,0:T(8,128)S(1)} %bitcast.166), channel_id=1, replica_groups=mesh['rows'=32,'cols'=16] {'cols'}, dimensions={1}, use_global_device_ids=true | all-gather | bytes 278528 | tf_op jit(solution)/shard_map/all_gather | solution.py:142
  213.8 104.8 %all-reduce = (f32[16]{0:T(128)S(1)}, f32[16]{0:T(128)S(1)}) all-reduce(f32[16]{0:T(128)S(1)} %get-tuple-element.305, f32[16]{0:T(128)S(1)} %multiply_reduce_fusion.5), channel_id=1, replica_groups=mesh['rows'=32,'cols'=16] {'rows','cols'}, use_global_device_ids=true, to_apply=%region_3.4 | all-reduce | flops 32 | bytes 256 | tf_op jit(solution)/shard_map/psum | solution.py:114
  319.2 94.7 %psum.45 = f32[16,256]{1,0:T(8,128)S(1)} all-reduce(f32[16,256]{1,0:T(8,128)S(1)} %fusion.82), channel_id=1, replica_groups=mesh['rows'=32,'cols'=16] {'rows','cols'}, use_global_device_ids=true, to_apply=%region_12.13 | all-reduce | flops 4096 | bytes 32768 | tf_op jit(solution)/shard_map/psum | solution.py:111
  414.5 95.5 %psum.46 = f32[16]{0:T(128)S(1)} all-reduce(f32[16]{0:T(128)S(1)} %get-tuple-element.307), channel_id=1, replica_groups=mesh['rows'=32,'cols'=16] {'rows','cols'}, use_global_device_ids=true, to_apply=%region_14.15 | all-reduce | flops 16 | bytes 128 | tf_op jit(solution)/shard_map/psum | solution.py:114
  510.0 18.0 %all_gather.14 = f32[16,4096]{1,0:T(8,128)S(1)} all-gather(f32[16,256]{1,0:T(8,128)S(1)} %get-tuple-element.308), channel_id=1, replica_groups=mesh['rows'=32,'cols'=16] {'cols'}, dimensions={1}, use_global_device_ids=true | all-gather | bytes 278528 | tf_op jit(solution)/shard_map/all_gather | solution.py:126
  528.2 1.7 collective-permute-start.9
  529.9 1.3 collective-permute-start.10
  531.2 0.7 collective-permute-done.9
  531.8 4.6 collective-permute-done.10
  536.5 12.0 %while.23 = (s32[]{:T(128)}, f32[16,2,128]{2,1,0:T(2,128)S(1)}, s32[]{:T(128)}, s32[2]{0:T(128)S(1)}, s32[]{:T(128)}, /*index=5*/f32[3,2,128]{2,0,1:T(4,128)S(1)...) while((s32[]{:T(128)}, f32[16,2,128]{2,1,0:T(2,128)S(1)}, ...), condition=%wide.region_18.19_spmd.clone, body=%wide.region_15.18_spmd.clone.sunk | while | flops 111156288 | bytes 6040561 | solution.py:84
  537.3 1.3 fusion.148
  538.5 0.8 gather_fusion.4
  539.3 0.7 fusion.150
  541.9 2.1 multiply_reduce_fusion.10
  544.0 4.3 fusion.151
  548.6 17.1 %all_gather.15 = f32[16,4096]{1,0:T(8,128)S(1)} all-gather(f32[16,256]{1,0:T(8,128)S(1)} %bitcast.167), channel_id=1, replica_groups=mesh['rows'=32,'cols'=16] {'cols'}, dimensions={1}, use_global_device_ids=true | all-gather | bytes 278528 | tf_op jit(solution)/shard_map/all_gather | solution.py:142
  565.9 105.4 %psum.47 = f32[16]{0:T(128)S(1)} all-reduce(f32[16]{0:T(128)S(1)} %multiply_reduce_fusion.3), channel_id=1, replica_groups=mesh['rows'=32,'cols'=16] {'rows','cols'}, use_global_device_ids=true, to_apply=%region_20.21 | all-reduce | flops 16 | bytes 128 | tf_op jit(solution)/shard_map/psum | solution.py:147
  671.2 0.9 multiply_subtract_fusion
  (78 shorter events, 8.3 us)
Async XLA Ops:
  0.6 159.0 %copy-start = (f32[256,256]{1,0:T(8,128)S(1)}, f32[256,256]{1,0:T(8,128)}, u32[]{:S(2)}) copy-start(f32[256,256]{1,0:T(8,128)} %param.15) | copy-start | bytes 786436
  0.6 45.6 %copy-start.1 = (f32[3,4096]{1,0:T(4,128)S(1)}, f32[3,4096]{1,0:T(4,128)}, u32[]{:S(2)}) copy-start(f32[3,4096]{1,0:T(4,128)} %param.10) | copy-start | bytes 147460
  0.7 8.5 %copy-start.4 = (s32[256]{0:T(256)S(1)}, s32[256]{0:T(256)}, u32[]{:S(2)}) copy-start(s32[256]{0:T(256)} %param.12) | copy-start | bytes 3076
  0.7 14.0 %copy-start.5 = (s32[32]{0:T(128)S(1)}, s32[32]{0:T(128)}, u32[]{:S(2)}) copy-start(s32[32]{0:T(128)} %param.14) | copy-start | bytes 388
  0.7 34.9 %copy-start.3 = (s32[32,18]{0,1:T(8,128)S(1)}, s32[32,18]{0,1:T(8,128)}, u32[]{:S(2)}) copy-start(s32[32,18]{0,1:T(8,128)} %param.13) | copy-start | bytes 6916
  1.5 179.2 %collective-permute-start.5 = (f32[3,1536]{1,0:T(4,128)S(1)}, f32[3,1536]{1,0:T(4,128)S(1)}, u32[]{:S(2)}, u32[]{:S(2)}) collective-permute-start(f32[3,1536]{1,0:T(4,128)S(1)} %get-tuple-element.298), channel_id=1, source_target_pairs={{0,16},{16,32},{32,48},{48,64},{64,80},{80,96},{96,112},{112,128},... | collective-permute-start | bytes 55304 | tf_op jit(solution)/shard_map/ppermute | solution.py:30
  6.3 174.4 %collective-permute-start.6 = (f32[3,1536]{1,0:T(4,128)S(1)}, f32[3,1536]{1,0:T(4,128)S(1)}, u32[]{:S(2)}, u32[]{:S(2)}) collective-permute-start(f32[3,1536]{1,0:T(4,128)S(1)} %get-tuple-element.299), channel_id=1, source_target_pairs={{16,0},{32,16},{48,32},{64,48},{80,64},{96,80},{112,96},{128,112},... | collective-permute-start | bytes 55304 | tf_op jit(solution)/shard_map/ppermute | solution.py:32
  7.6 49.3 %copy-start.2 = (f32[16,4096]{1,0:T(8,128)S(1)}, f32[16,4096]{1,0:T(8,128)}, u32[]{:S(2)}) copy-start(f32[16,4096]{1,0:T(8,128)} %param.11) | copy-start | bytes 786436
  10.1 7.0 %collective-permute-start = (f32[3,256]{0,1:T(8,128)S(1)}, f32[3,256]{0,1:T(8,128)S(1)}, u32[]{:S(2)}, u32[]{:S(2)}) collective-permute-start(f32[3,256]{0,1:T(8,128)S(1)} %multiply_bitcast_fusion), channel_id=1, source_target_pairs={{0,16},{16,0},{32,48},{48,32},{64,80},{80,64},{96,112},{112,96},{1... | collective-permute-start | bytes 9224 | tf_op jit(solution)/shard_map/ppermute | solution.py:17
  17.2 13.7 %collective-permute-start.1 = (f32[3,256]{0,1:T(8,128)S(1)}, f32[3,256]{0,1:T(8,128)S(1)}, u32[]{:S(2)}, u32[]{:S(2)}) collective-permute-start(f32[3,256]{0,1:T(8,128)S(1)} %fusion.108), channel_id=1, source_target_pairs={{0,32},{16,48},{32,0},{48,16},{64,96},{80,112},{96,64},{112,80},{1... | collective-permute-start | bytes 9224 | tf_op jit(solution)/shard_map/ppermute | solution.py:17
  30.9 12.5 %collective-permute-start.2 = (f32[3,256]{0,1:T(8,128)S(1)}, f32[3,256]{0,1:T(8,128)S(1)}, u32[]{:S(2)}, u32[]{:S(2)}) collective-permute-start(f32[3,256]{0,1:T(8,128)S(1)} %add.208), channel_id=1, source_target_pairs={{0,64},{16,80},{32,96},{48,112},{64,0},{80,16},{96,32},{112,48},{1... | collective-permute-start | bytes 9224 | tf_op jit(solution)/shard_map/ppermute | solution.py:17
  43.4 5.7 collective-permute-start.3
  49.1 7.5 %collective-permute-start.4 = (f32[3,256]{0,1:T(8,128)S(1)}, f32[3,256]{0,1:T(8,128)S(1)}, u32[]{:S(2)}, u32[]{:S(2)}) collective-permute-start(f32[3,256]{0,1:T(8,128)S(1)} %add.210), channel_id=1, source_target_pairs={{0,256},{16,272},{32,288},{48,304},{64,320},{80,336},{96,352},{112... | collective-permute-start | bytes 9224 | tf_op jit(solution)/shard_map/ppermute | solution.py:17
  176.7 4.7 collective-permute-start.7
  179.4 5.8 collective-permute-start.8
  528.2 3.6 collective-permute-start.9
  529.9 6.6 collective-permute-start.10
